TPU v7x, 32 devices: a whole 2x2x4 slice. The times are simulated.
32 devices in a mesh: tok: 16 (over z, y, x), head: 2 (over core).
Axes of the slice: x: 2, y: 2, z: 4, core: 2. Of those that a mesh axis runs over, the one named last changes fastest.
Arguments:
- queries: bfloat16 [2, 4096, 512], P('head', 'tok'), may hold values from -6 to 6
- key_rows: bfloat16 [2, 4096, 512], P('head', 'tok'), may hold values from -6 to 6
- value_rows: bfloat16 [2, 4096, 512], P('head', 'tok'), may hold values from -6 to 6
- step_rates: float32 [2, 4096], P('head', 'tok'), may hold values from 0.1 to 1
- w_gate: bfloat16 [2, 512, 512], P('head'), may hold values from -0.25 to 0.25
- w_up: bfloat16 [2, 512, 512], P('head'), may hold values from -0.25 to 0.25
- w_down: bfloat16 [2, 512, 512], P('head'), may hold values from -0.25 to 0.25
- out_gain: float32 [2, 512], P('head'), may hold values from 0.1 to 1.9
- cotangent: bfloat16 [2, 4096, 512], P('head', 'tok'), may hold values from -6 to 6
Outputs:
- grad_queries: bfloat16 [2, 4096, 512], P('head', 'tok')
- grad_keys: bfloat16 [2, 4096, 512], P('head', 'tok')
- grad_values: bfloat16 [2, 4096, 512], P('head', 'tok')
- grad_gate: float32 [2, 512, 512], P('head', 'tok')
- grad_up: float32 [2, 512, 512], P('head', 'tok')
- grad_down: float32 [2, 512, 512], P('head', 'tok')
All inputs are finite; a program needn't handle non-finite values.
Results may differ from a plain program's by a relative error of at most 0.03.
Values sent between devices are 32-bit elements; how exact they have to be, the bound alone decides.
A program may use at most 128 MiB of HBM per device.

v0:
```python
import jax
import jax.numpy as jnp
from jax import lax
from jax.experimental import pallas as pl
from jax.experimental.pallas import tpu as pltpu
from jax.sharding import PartitionSpec as P

NS_STEPS = 3
WAVE = 3
AHEAD = 1


coef_first = 3.4445
coef_second = -4.775
coef_third = 2.0315
inner_step = 0.5


def silu_parts(pre_gate):
    sigma_gate = jax.nn.sigmoid(pre_gate)
    act_gate = pre_gate * sigma_gate
    slope_gate = sigma_gate * (1.0 + pre_gate * (1.0 - sigma_gate))
    return (act_gate, slope_gate, sigma_gate)


def mxu(first_op, second_op, first_dim, second_dim):
    return lax.dot_general(
        first_op,
        second_op,
        (((first_dim,), (second_dim,)), ((), ())),
        preferred_element_type=jnp.float32,
    )


def unitary_forward(inner_grads, weights):
    size = weights[0].shape[0]
    count = len(weights)

    def kernel(*refs):
        matrices, olds = refs[:count], refs[count : 2 * count]
        new_ref, narrow_ref, gram_ref, poly_ref, current = refs[2 * count :]
        for which in range(count):

            @pl.when(pl.program_id(0) == which)
            def _(which=which):
                matrix = matrices[which][...]
                current[...] = matrix / jnp.sqrt(jnp.sum(matrix * matrix) + 1e-06)

        def step(iteration, carry):
            narrow = current[...].astype(jnp.bfloat16)
            narrow_ref[0, iteration] = narrow
            gram = mxu(narrow, narrow, 1, 1)
            gram_low = gram.astype(jnp.bfloat16)
            gram_ref[0, iteration] = gram_low
            poly = (coef_second * gram + coef_third * mxu(gram_low, gram_low, 1, 0)).astype(
                jnp.bfloat16
            )
            poly_ref[0, iteration] = poly
            current[...] = coef_first * current[...] + mxu(poly, narrow, 1, 0)
            return carry

        lax.fori_loop(0, NS_STEPS, step, 0)
        for which in range(count):

            @pl.when(pl.program_id(0) == which)
            def _(which=which):
                old = olds[which][...].astype(jnp.float32)
                new_ref[0] = (old - inner_step * current[...]).astype(jnp.bfloat16)

    vmem = pl.BlockSpec(memory_space=pltpu.VMEM)
    saved = jax.ShapeDtypeStruct((count, NS_STEPS, size, size), jnp.bfloat16)
    saved_spec = pl.BlockSpec((1, NS_STEPS, size, size), lambda i: (i, 0, 0, 0))
    return pl.pallas_call(
        kernel,
        grid=(count,),
        out_shape=[jax.ShapeDtypeStruct((count, size, size), jnp.bfloat16), saved, saved, saved],
        in_specs=[vmem] * (2 * count),
        out_specs=[pl.BlockSpec((1, size, size), lambda i: (i, 0, 0))] + [saved_spec] * 3,
        scratch_shapes=[pltpu.VMEM((size, size), jnp.float32)],
        name="unitary_forward",
    )(*inner_grads, *weights)


def unitary_backward(inner_grads, outer_grads, saved):
    size = inner_grads[0].shape[0]
    count = len(inner_grads)

    def kernel(*refs):
        matrices, outers = refs[:count], refs[count : 2 * count]
        narrow_ref, gram_ref, poly_ref, cot_ref, grad = refs[2 * count :]
        for which in range(count):

            @pl.when(pl.program_id(0) == which)
            def _(which=which):
                grad[...] = -inner_step * outers[which][...]

        def step(back_iteration, carry):
            iteration = NS_STEPS - 1 - back_iteration
            narrow = narrow_ref[0, iteration]
            gram_low = gram_ref[0, iteration]
            grad_low = grad[...].astype(jnp.bfloat16)
            poly_grad = mxu(grad_low, narrow, 1, 1).astype(jnp.bfloat16).astype(jnp.float32)
            pair = poly_grad + poly_grad.T
            product = mxu(pair.astype(jnp.bfloat16), gram_low, 1, 0)
            gram_grad = coef_second * pair + coef_third * (product + product.T)
            narrow_grad = mxu(poly_ref[0, iteration], grad_low, 0, 0) + mxu(
                gram_grad.astype(jnp.bfloat16), narrow, 1, 0
            )
            grad[...] = coef_first * grad[...] + narrow_grad.astype(jnp.bfloat16).astype(
                jnp.float32
            )
            return carry

        lax.fori_loop(0, NS_STEPS, step, 0)
        for which in range(count):

            @pl.when(pl.program_id(0) == which)
            def _(which=which):
                matrix = matrices[which][...]
                inverse = lax.rsqrt(jnp.sum(matrix * matrix) + 1e-06)
                along = jnp.sum(matrix * grad[...]) * inverse * inverse * inverse
                cot_ref[0] = (grad[...] * inverse - matrix * along).astype(jnp.bfloat16)

    vmem = pl.BlockSpec(memory_space=pltpu.VMEM)
    saved_spec = pl.BlockSpec((1, NS_STEPS, size, size), lambda i: (i, 0, 0, 0))
    return pl.pallas_call(
        kernel,
        grid=(count,),
        out_shape=jax.ShapeDtypeStruct((count, size, size), jnp.bfloat16),
        in_specs=[vmem] * (2 * count) + [saved_spec] * 3,
        out_specs=pl.BlockSpec((1, size, size), lambda i: (i, 0, 0)),
        scratch_shapes=[pltpu.VMEM((size, size), jnp.float32)],
        name="unitary_backward",
    )(*inner_grads, *outer_grads, *saved)


def on_core(kernel, name, outs, *operands):
    vmem = pl.BlockSpec(memory_space=pltpu.VMEM)
    return pl.pallas_call(
        kernel,
        out_shape=[jax.ShapeDtypeStruct(shape, kind) for shape, kind in outs],
        in_specs=[vmem] * len(operands),
        out_specs=[vmem] * len(outs),
        name=name,
    )(*operands)


def key_forward(w_gate, w_up, w_down, key_rows, value_rows, step_rates):
    def kernel(gate_w, up_w, down_w, keys, values, rates, a, b, c, gate, up, mid, mixed, target, dgate, dup):
        rows = keys[...]
        key_gate = mxu(rows, gate_w[...], 1, 0)
        key_up = mxu(rows, up_w[...], 1, 0)
        aim = (-rates[...] * values[...].astype(jnp.float32)).astype(jnp.bfloat16)
        key_mid = mxu(aim, down_w[...], 1, 1)
        act_gate, slope_gate, _ = silu_parts(key_gate)
        gate[...] = key_gate
        up[...] = key_up
        mid[...] = key_mid
        target[...] = aim
        mixed[...] = (act_gate * key_up).astype(jnp.bfloat16)
        dgate[...] = (key_mid * key_up * slope_gate).astype(jnp.bfloat16)
        dup[...] = (key_mid * act_gate).astype(jnp.bfloat16)
        a[...] = mxu(rows, dgate[...], 0, 0)
        b[...] = mxu(rows, dup[...], 0, 0)
        c[...] = mxu(mixed[...], target[...], 0, 0)

    square = (w_gate.shape, jnp.float32)
    wide, narrow = (key_rows.shape, jnp.float32), (key_rows.shape, jnp.bfloat16)
    results = on_core(
        kernel,
        "key_forward",
        [square] * 3 + [wide] * 3 + [narrow] * 4,
        w_gate,
        w_up,
        w_down,
        key_rows,
        value_rows,
        step_rates[:, None],
    )
    return results[:3], results[3:]


def key_backward(w_gate, w_up, w_down, key_rows, step_rates, stored, cots):
    def kernel(
        gate_w, up_w, down_w, keys, rates, gate, up, mid, mixed, target, dgate, dup, cots,
        key_grad, value_grad, a, b, c, mid_low, gate_low, up_low,
    ):
        rows = keys[...]
        back_gate = mxu(rows, cots[0], 1, 0)
        back_up = mxu(rows, cots[1], 1, 0)
        back_mixed = mxu(target[...], cots[2], 1, 1)
        key_gate, key_up, key_mid = gate[...], up[...], mid[...]
        act_gate, slope_gate, sigma_gate = silu_parts(key_gate)
        curve_gate = (
            sigma_gate * (1.0 - sigma_gate) * (2.0 + key_gate * (1.0 - 2.0 * sigma_gate))
        )
        mid_low[...] = (back_gate * key_up * slope_gate + back_up * act_gate).astype(jnp.bfloat16)
        gate_low[...] = (
            back_gate * key_mid * key_up * curve_gate
            + back_up * key_mid * slope_gate
            + back_mixed * key_up * slope_gate
        ).astype(jnp.bfloat16)
        up_low[...] = (back_gate * key_mid * slope_gate + back_mixed * act_gate).astype(
            jnp.bfloat16
        )
        a[...] = mxu(rows, gate_low[...], 0, 0)
        b[...] = mxu(rows, up_low[...], 0, 0)
        c[...] = mxu(mid_low[...], target[...], 0, 0)
        key_grad[...] = (
            mxu(dgate[...], cots[0], 1, 1)
            + mxu(dup[...], cots[1], 1, 1)
            + mxu(gate_low[...], gate_w[...], 1, 1)
            + mxu(up_low[...], up_w[...], 1, 1)
        ).astype(jnp.bfloat16)
        value_sum = mxu(mixed[...], cots[2], 1, 0) + mxu(mid_low[...], down_w[...], 1, 0)
        value_grad[...] = (-rates[...] * value_sum).astype(jnp.bfloat16)

    square = (w_gate.shape, jnp.float32)
    narrow = (key_rows.shape, jnp.bfloat16)
    results = on_core(
        kernel,
        "key_backward",
        [narrow] * 2 + [square] * 3 + [narrow] * 3,
        w_gate,
        w_up,
        w_down,
        key_rows,
        step_rates[:, None],
        *stored,
        cots,
    )
    return results[0], results[1], results[2:5]


def query_forward(news, queries, out_gain, cotangent):
    def kernel(news, rows, gain, cot, sums, gate, up, mixed, output):
        query_gate = mxu(rows[...], news[0], 1, 0)
        query_up = mxu(rows[...], news[1], 1, 0)
        gate[...] = query_gate
        up[...] = query_up
        act_gate, _, _ = silu_parts(query_gate)
        mixed[...] = (act_gate * query_up).astype(jnp.bfloat16)
        out = mxu(mixed[...], news[2], 1, 0)
        output[...] = out
        squares = jnp.sum(out * out, axis=1, keepdims=True)
        aligned = jnp.sum(cot[...].astype(jnp.float32) * gain[...] * out, axis=1, keepdims=True)
        lane = lax.broadcasted_iota(jnp.int32, sums.shape, 1)
        sums[...] = jnp.where(lane < sums.shape[1] // 2, squares, aligned)

    wide, narrow = (queries.shape, jnp.float32), (queries.shape, jnp.bfloat16)
    results = on_core(
        kernel,
        "query_forward",
        [((queries.shape[0], 128), jnp.float32), wide, wide, narrow, wide],
        news,
        queries,
        out_gain,
        cotangent,
    )
    return results[0], results[1:]


def query_backward(news, queries, out_gain, cotangent, sums, stored, full_width):
    def kernel(news, rows, gain, cot, sums, gate, up, mixed, output, query_grad, a, b, c, grad, dgate, dup):
        squares = sums[:, :1]
        aligned = sums[:, sums.shape[1] // 2 : sums.shape[1] // 2 + 1]
        inverse_rms = lax.rsqrt(squares / full_width + 1e-05)
        pull = aligned * inverse_rms * inverse_rms * inverse_rms / full_width
        grad[...] = (
            gain[...] * cot[...].astype(jnp.float32) * inverse_rms - output[...] * pull
        ).astype(jnp.bfloat16)
        query_mid = mxu(grad[...], news[2], 1, 1)
        act_gate, slope_gate, _ = silu_parts(gate[...])
        dgate[...] = (query_mid * up[...] * slope_gate).astype(jnp.bfloat16)
        dup[...] = (query_mid * act_gate).astype(jnp.bfloat16)
        a[...] = mxu(rows[...], dgate[...], 0, 0)
        b[...] = mxu(rows[...], dup[...], 0, 0)
        c[...] = mxu(mixed[...], grad[...], 0, 0)
        query_grad[...] = (
            mxu(dgate[...], news[0], 1, 1) + mxu(dup[...], news[1], 1, 1)
        ).astype(jnp.bfloat16)

    square = (news.shape[1:], jnp.float32)
    narrow = (queries.shape, jnp.bfloat16)
    results = on_core(
        kernel,
        "query_backward",
        [narrow] + [square] * 3 + [narrow] * 3,
        news,
        queries,
        out_gain,
        cotangent,
        sums,
        *stored,
    )
    return results[0], results[1:4]


def bit_orders(bits):
    plain = tuple(range(bits))
    if bits < 3:
        return (plain, plain[::-1])
    swapped = (1, 0) + plain[2:]
    return (plain, swapped, (2, 0, 1) + plain[3:], plain, swapped, (2, 1, 0) + plain[3:])


def sum_over_tok(arrays, devices, call_id, whole):
    bits = devices.bit_length() - 1
    rows, columns = arrays[0].shape
    block = rows // devices
    width = 128
    count = len(arrays)
    orders = bit_orders(bits)
    streams = [
        (array, pl.ds(start, width))
        for array in range(count)
        for start in range(0, columns, width)
    ]
    split = (2,) * bits + (block,)

    def kernel(*refs):
        given = refs[:count]
        shares = refs[count : 2 * count]
        position = 2 * count
        wholes = refs[position : position + count] if whole else ()
        position += len(wholes)
        partial = refs[position : position + count]
        landing = refs[position + count : position + count + bits]
        sems = refs[position + count + bits :]
        me = lax.axis_index("tok")
        mine = [lax.rem(lax.div(me, 1 << bit), 2) for bit in range(bits)]
        partner = [me + (1 - 2 * mine[bit]) * (1 << bit) for bit in range(bits)]

        barrier = pltpu.get_barrier_semaphore()
        for bit in range(bits):
            pl.semaphore_signal(
                barrier,
                inc=1,
                device_id={"tok": partner[bit]},
                device_id_type=pl.DeviceIdType.MESH,
            )
        pl.semaphore_wait(barrier, bits)

        def pick(fixed, lanes):
            leading = tuple(fixed.get(bit, slice(None)) for bit in reversed(range(bits)))
            return leading + (slice(None), lanes)

        sent = []

        def send(source, target, stream, stage, phase, bit):
            copy = pltpu.make_async_remote_copy(
                src_ref=source,
                dst_ref=target,
                send_sem=sems[2 * phase].at[stream, stage],
                recv_sem=sems[2 * phase + 1].at[stream, stage],
                device_id={"tok": partner[bit]},
                device_id_type=pl.DeviceIdType.MESH,
            )
            copy.start()
            sent.append(copy)
            return copy

        def halve(stream, stage):
            array, lanes = streams[stream]
            order = orders[stream % len(orders)]
            fixed = {bit: mine[bit] for bit in order[:stage]}
            bit = order[stage]
            fixed[bit] = 1 - mine[bit]
            held = given[array] if stage == 0 else partial[array]
            return send(
                held.at[pick(fixed, lanes)], landing[stage].at[stream], stream, stage, 0, bit
            )

        def double(stream, stage):
            array, lanes = streams[stream]
            order = orders[stream % len(orders)]
            region = wholes[array].at[pick({bit: mine[bit] for bit in order[: stage + 1]}, lanes)]
            return send(region, region, stream, stage, 1, order[stage])

        flying = {}

        def advance(stream, step):
            array, lanes = streams[stream]
            order = orders[stream % len(orders)]
            if step > 0:
                flying[stream].wait_recv()
            if 0 < step <= bits:
                stage = step - 1
                kept = pick({bit: mine[bit] for bit in order[:step]}, lanes)
                held = given[array] if stage == 0 else partial[array]
                total = held[kept] + landing[stage][stream]
                if step < bits:
                    partial[array][kept] = total
                else:
                    shares[array][:, lanes] = total
                    if whole:
                        wholes[array][kept] = total
            if step < bits:
                flying[stream] = halve(stream, step)
            elif step < steps:
                flying[stream] = double(stream, 2 * bits - 1 - step)

        steps = 2 * bits if whole else bits
        waves = [range(first, min(first + WAVE, len(streams))) for first in range(0, len(streams), WAVE)]
        begins = [max(0, wave - AHEAD) for wave in range(len(waves))]
        for tick in range(begins[-1] + steps + 1):
            for begin, wave in zip(begins, waves):
                if 0 <= tick - begin <= steps:
                    for stream in wave:
                        advance(stream, tick - begin)
        for copy in sent:
            copy.wait_send()

    phases = 2 if whole else 1
    outs = [jax.ShapeDtypeStruct((block, columns), jnp.float32)] * count
    if whole:
        outs += [jax.ShapeDtypeStruct(split + (columns,), jnp.float32)] * count
    vmem = pl.BlockSpec(memory_space=pltpu.VMEM)
    results = pl.pallas_call(
        kernel,
        out_shape=outs,
        in_specs=[vmem] * count,
        out_specs=[vmem] * len(outs),
        scratch_shapes=[pltpu.VMEM(split + (columns,), jnp.float32)] * count
        + [
            pltpu.VMEM((len(streams),) + (2,) * (bits - 1 - stage) + (block, width), jnp.float32)
            for stage in range(bits)
        ]
        + [pltpu.SemaphoreType.DMA((len(streams), bits))] * (2 * phases),
        compiler_params=pltpu.CompilerParams(collective_id=call_id, has_side_effects=True),
        name="sum_whole" if whole else "sum_share",
    )(*[array.reshape(split + (columns,)) for array in arrays])
    shares = results[:count]
    return shares, [array.reshape(rows, columns) for array in results[count:]]


def local(queries, key_rows, value_rows, step_rates, w_gate, w_up, w_down, out_gain, cotangent):
    heads_here, _, head_size = queries.shape
    assert heads_here == 1
    queries, key_rows, value_rows, step_rates, w_gate, w_up, w_down, cotangent = (
        array[0]
        for array in (
            queries, key_rows, value_rows, step_rates, w_gate, w_up, w_down, cotangent,
        )
    )
    devices = lax.axis_size("tok")
    full_width = lax.axis_size("head") * head_size
    local_grads, stored = key_forward(w_gate, w_up, w_down, key_rows, value_rows, step_rates)
    inner_grads = sum_over_tok(local_grads, devices, 0, True)[1]
    news, *saved = unitary_forward(inner_grads, (w_gate, w_up, w_down))
    sums, query_stored = query_forward(news, queries, out_gain, cotangent)
    sums = lax.psum(sums, "head")
    query_grad, query_terms = query_backward(
        news, queries, out_gain, cotangent, sums, query_stored, full_width
    )
    query_shares, outer_grads = sum_over_tok(query_terms, devices, 1, True)
    cots = unitary_backward(inner_grads, outer_grads, saved)
    key_grad, value_grad, key_terms = key_backward(
        w_gate, w_up, w_down, key_rows, step_rates, stored, cots
    )
    key_shares, _ = sum_over_tok(key_terms, devices, 2, False)
    return (query_grad[None], key_grad[None], value_grad[None]) + tuple(
        (query_share + key_share)[None] for query_share, key_share in zip(query_shares, key_shares)
    )


def solution(mesh):
    in_specs = (
        P("head", "tok", None),
        P("head", "tok", None),
        P("head", "tok", None),
        P("head", "tok"),
        P("head", None, None),
        P("head", None, None),
        P("head", None, None),
        P("head", None),
        P("head", "tok", None),
    )
    out_specs = (
        P("head", "tok", None),
        P("head", "tok", None),
        P("head", "tok", None),
        P("head", "tok", None),
        P("head", "tok", None),
        P("head", "tok", None),
    )
    return jax.shard_map(local, mesh=mesh, in_specs=in_specs, out_specs=out_specs, check_vma=False)
```

profile of v0, /device:TPU:0, one launch (start us, length us, event | category | flops | bytes accessed | tf_op | source)
XLA Modules:
  0.0 258.7 jit_solution(4402168555844537658)
XLA Ops:
  7.2 0.0 all-reduce.2.cloned.1.call-start
  7.2 1.5 copy.15.rates
  8.7 4.6 %key_forward.1 = (f32[512,512]{1,0:T(8,128)}, f32[512,512]{1,0:T(8,128)}, f32[512,512]{1,0:T(8,128)}, f32[256,512]{1,0:T(8,128)}, f32[256,512]{1,0:T(8,128)}, /*...) custom-call(bf16[512,512]{1,0:T(8,128)(2,1)} %bitcast.32, ...), custom_call_target="tpu_custom_call" | custom-call | tf_op jit(solution)/shard_map/key_forward/pallas_call | solution.py:139
  13.3 65.9 %sum_whole.2 = (f32[32,512]{1,0:T(8,128)}, f32[32,512]{1,0:T(8,128)}, f32[32,512]{1,0:T(8,128)}, f32[2,2,2,2,32,512]{5,4,3,2,1,0:T(8,128)}, f32[2,2,2,2,32,512]{...) custom-call(f32[2,2,2,2,32,512]{5,4,3,2,1,0:T(8,128)} %bitcast.53, f32[2,2,2,2,32,512]{5,4,3,2,1,0:T(8,128)} %bitcast.54, ...), custom_call_target="tpu_custom_call" | custom-call | tf_op jit(solution)/shard_map/sum_whole/pallas_call | solution.py:419
  79.2 17.0 %unitary_forward.1 = (bf16[3,512,512]{2,1,0:T(8,128)(2,1)}, bf16[3,3,512,512]{3,2,1,0:T(8,128)(2,1)}, bf16[3,3,512,512]{3,2,1,0:T(8,128)(2,1)}, bf16[3,3,512,512]{3,2,1,0:T(8,128)(2,1)}) custom-call(f32[512,512]{1,0:T(8,128)} %bitcast.41, f32[512,512]{1,0:T(8,128)} %bitcast.43, f32[512,512]{1,0:T(8,128)} %bitcast.45, bf16[512,512]{1,0:T(8,128)(2,1)} %bitcast.33, ...), custom_call_target="tpu_custom_call" | custom-call | tf_op jit(solution)/shard_map/unitary_forward/pallas_call | solution.py:73
  96.2 3.1 %query_forward.1 = (f32[256,128]{1,0:T(8,128)}, f32[256,512]{1,0:T(8,128)}, f32[256,512]{1,0:T(8,128)}, bf16[256,512]{1,0:T(8,128)(2,1)}, f32[256,512]{1,0:T(8,128)}) custom-call(bf16[3,512,512]{2,1,0:T(8,128)(2,1)} %get-tuple-element.52.news, bf16[256,512]{1,0:T(8,128)(2,1)} %bitcast.56, f32[1,512]{1,0:T(1,128)} %gain.3, bf16[256,512]{1,0:T(8,128)(2,1)} %bitcast.58), custom_call_target="tpu_custom_call" | custom-call | tf_op jit(solution)/shard_map/query_forward/pallas_call | solution.py:139
  99.3 0.0 all-reduce.2.cloned.1.call-update
  99.3 16.5 %all-reduce.2.cloned.1.call-done.sums = f32[256,128]{1,0:T(8,128)} async-done(((f32[256,128]{1,0:T(8,128)}), f32[256,128]{1,0:T(8,128)}) %all-reduce.2.cloned.1.call-update) | async-done | bytes 131088 | tf_op jit(solution)/shard_map/psum | solution.py:452
  115.9 4.7 %query_backward.1 = (bf16[256,512]{1,0:T(8,128)(2,1)}, f32[512,512]{1,0:T(8,128)}, f32[512,512]{1,0:T(8,128)}, f32[512,512]{1,0:T(8,128)}, bf16[256,512]{1,0:T(8...) custom-call(bf16[3,512,512]{2,1,0:T(8,128)(2,1)} %get-tuple-element.52.news, bf16[256,512]{1,0:T(8,128)(2,1)} %bitcast.57, ...), custom_call_target="tpu_custom_call" | custom-call | tf_op jit(solution)/shard_map/query_backward/pallas_call | solution.py:139
  120.6 65.1 %sum_whole.3 = (f32[32,512]{1,0:T(8,128)}, f32[32,512]{1,0:T(8,128)}, f32[32,512]{1,0:T(8,128)}, f32[2,2,2,2,32,512]{5,4,3,2,1,0:T(8,128)}, f32[2,2,2,2,32,512]{...) custom-call(f32[2,2,2,2,32,512]{5,4,3,2,1,0:T(8,128)} %bitcast.50, f32[2,2,2,2,32,512]{5,4,3,2,1,0:T(8,128)} %bitcast.51, ...), custom_call_target="tpu_custom_call" | custom-call | tf_op jit(solution)/shard_map/sum_whole/pallas_call | solution.py:419
  185.7 21.6 %unitary_backward.1.cots = bf16[3,512,512]{2,1,0:T(8,128)(2,1)} custom-call(f32[512,512]{1,0:T(8,128)} %bitcast.42, f32[512,512]{1,0:T(8,128)} %bitcast.44, f32[512,512]{1,0:T(8,128)} %bitcast.46, f32[512,512]{1,0:T(8,128)} %bitcast.62, f32[512,512]{1,0:T(8,128)} %bitcast.63, f32[512,512]{1,0:T(8,128)} %bitcast.64, ...), custom_call_target="tpu_custom_call" | custom-call | tf_op jit(solution)/shard_map/unitary_backward/pallas_call | solution.py:126
  207.3 0.0 copy-start
  207.3 0.0 copy-start.1
  207.3 0.0 copy-start.2
  207.3 6.2 %key_backward.1 = (bf16[256,512]{1,0:T(8,128)(2,1)}, bf16[256,512]{1,0:T(8,128)(2,1)}, f32[512,512]{1,0:T(8,128)}, f32[512,512]{1,0:T(8,128)}, f32[512,512]{1,0:...) custom-call(bf16[512,512]{1,0:T(8,128)(2,1)} %bitcast.34, ...), custom_call_target="tpu_custom_call" | custom-call | tf_op jit(solution)/shard_map/key_backward/pallas_call | solution.py:139
  213.5 35.2 %sum_share.1 = (f32[32,512]{1,0:T(8,128)}, f32[32,512]{1,0:T(8,128)}, f32[32,512]{1,0:T(8,128)}) custom-call(f32[2,2,2,2,32,512]{5,4,3,2,1,0:T(8,128)} %bitcast.47, f32[2,2,2,2,32,512]{5,4,3,2,1,0:T(8,128)} %bitcast.48, f32[2,2,2,2,32,512]{5,4,3,2,1,0:T(8,128)} %bitcast.49), custom_call_target="tpu_custom_call" | custom-call | tf_op jit(solution)/shard_map/sum_share/pallas_call | solution.py:419
  248.8 0.0 copy-done
  248.8 1.5 add_bitcast_fusion.2
  250.3 0.0 copy-done.1
  250.3 0.0 copy-done.2
  250.3 1.5 add_bitcast_fusion
Async XLA Ops:
  7.2 108.7 %all-reduce.2.cloned.1.call-start = ((), (), s32[]{:S(2)}) async-start(), calls=%async_computation | async-start | bytes 262144 | tf_op jit(solution)/shard_map/psum | solution.py:452
  207.3 41.5 %copy-start = (f32[32,512]{1,0:T(8,128)S(1)}, f32[32,512]{1,0:T(8,128)}, u32[]{:S(2)}) copy-start(f32[32,512]{1,0:T(8,128)} %get-tuple-element.77) | copy-start | bytes 196612
  207.3 43.0 %copy-start.1 = (f32[32,512]{1,0:T(8,128)S(1)}, f32[32,512]{1,0:T(8,128)}, u32[]{:S(2)}) copy-start(f32[32,512]{1,0:T(8,128)} %get-tuple-element.82) | copy-start | bytes 196612
  207.3 43.0 %copy-start.2 = (f32[32,512]{1,0:T(8,128)S(1)}, f32[32,512]{1,0:T(8,128)}, u32[]{:S(2)}) copy-start(f32[32,512]{1,0:T(8,128)} %get-tuple-element.84) | copy-start | bytes 196612
Sparse Core Ops, SparseCore 0:
  99.4 16.3 all-reduce.1
where the time goes:
time: 259 us
  Pallas kernels  223 us (86%)
  waiting for transfers between devices  16.6 us (6%)
  between operations  14.1 us (5%)
  other arithmetic  3.01 us (1%)
    pallas_call x3, Pallas kernels, sum_over_tok(): pl.pallas_call(kernel, out_shape=outs, in_specs=[vmem] * count, out_specs...  166 us
    pallas_call x1, Pallas kernels, unitary_backward(): pl.pallas_call(kernel, grid=(count,), out_shape=jax.ShapeDtypeStruct((cou...  21.6 us
    pallas_call x4, Pallas kernels, on_core(): pl.pallas_call(kernel, out_shape=[jax.ShapeDtypeStruct(shape, kind) for s...  18.7 us
    pallas_call x1, Pallas kernels, unitary_forward(): pl.pallas_call(kernel, grid=(count,), out_shape=[jax.ShapeDtypeStruct((co...  17 us
    psum x1, waiting for transfers between devices, local(): sums = lax.psum(sums, 'head')  16.5 us
  transfers between devices with their start and end apart: 1, of which 1 were waited for; matrix products, arithmetic and copies ran while one was open for 0% of the time, Pallas kernels for 0%

commit v1 on v0

--- a/solution.py
+++ b/solution.py
@@ -6,8 +6,8 @@
 from jax.sharding import PartitionSpec as P
 
 NS_STEPS = 3
-WAVE = 3
-AHEAD = 1
+WAVE = 12
+AHEAD = 0
 
 
 coef_first = 3.4445
@@ -296,15 +296,61 @@
     return results[0], results[1:4]
 
 
+def sum_over_pair(partial, devices, call_id):
+    others = devices - 1
+
+    def kernel(given, total, landing, send_sems, recv_sems):
+        me = lax.axis_index("head")
+        peers = [lax.rem(me + step + 1, devices) for step in range(others)]
+        barrier = pltpu.get_barrier_semaphore()
+        for peer in peers:
+            pl.semaphore_signal(
+                barrier, inc=1, device_id={"head": peer}, device_id_type=pl.DeviceIdType.MESH
+            )
+        pl.semaphore_wait(barrier, others)
+        copies = []
+        for step, peer in enumerate(peers):
+            copy = pltpu.make_async_remote_copy(
+                src_ref=given,
+                dst_ref=landing.at[step],
+                send_sem=send_sems.at[step],
+                recv_sem=recv_sems.at[step],
+                device_id={"head": peer},
+                device_id_type=pl.DeviceIdType.MESH,
+            )
+            copy.start()
+            copies.append(copy)
+        result = given[...]
+        for step, copy in enumerate(copies):
+            copy.wait_recv()
+            result = result + landing[step]
+        total[...] = result
+        for copy in copies:
+            copy.wait_send()
+
+    vmem = pl.BlockSpec(memory_space=pltpu.VMEM)
+    return pl.pallas_call(
+        kernel,
+        out_shape=jax.ShapeDtypeStruct(partial.shape, jnp.float32),
+        in_specs=[vmem],
+        out_specs=vmem,
+        scratch_shapes=[pltpu.VMEM((others,) + partial.shape, jnp.float32)]
+        + [pltpu.SemaphoreType.DMA((others,))] * 2,
+        compiler_params=pltpu.CompilerParams(collective_id=call_id, has_side_effects=True),
+        name="sum_pair",
+    )(partial)
+
+
 def bit_orders(bits):
     plain = tuple(range(bits))
     if bits < 3:
         return (plain, plain[::-1])
-    swapped = (1, 0) + plain[2:]
-    return (plain, swapped, (2, 0, 1) + plain[3:], plain, swapped, (2, 1, 0) + plain[3:])
-
-
-def sum_over_tok(arrays, devices, call_id, whole):
+    if bits == 4:
+        return (plain, (0, 2, 1, 3), (1, 0, 3, 2), (1, 3, 0, 2), (2, 0, 1, 3), (3, 1, 0, 2))
+    return tuple(plain[turn:] + plain[:turn] for turn in range(bits))
+
+
+def sum_over_tok(arrays, devices, call_id, whole, added=()):
     bits = devices.bit_length() - 1
     rows, columns = arrays[0].shape
     block = rows // devices
@@ -320,8 +366,10 @@
 
     def kernel(*refs):
         given = refs[:count]
-        shares = refs[count : 2 * count]
-        position = 2 * count
+        addends = refs[count : count + len(added)]
+        position = count + len(added)
+        shares = refs[position : position + count]
+        position += count
         wholes = refs[position : position + count] if whole else ()
         position += len(wholes)
         partial = refs[position : position + count]
@@ -392,7 +440,7 @@
                 if step < bits:
                     partial[array][kept] = total
                 else:
-                    shares[array][:, lanes] = total
+                    shares[array][:, lanes] = total + addends[array][:, lanes] if added else total
                     if whole:
                         wholes[array][kept] = total
             if step < bits:
@@ -419,7 +467,7 @@
     results = pl.pallas_call(
         kernel,
         out_shape=outs,
-        in_specs=[vmem] * count,
+        in_specs=[vmem] * (count + len(added)),
         out_specs=[vmem] * len(outs),
         scratch_shapes=[pltpu.VMEM(split + (columns,), jnp.float32)] * count
         + [
@@ -429,7 +477,7 @@
         + [pltpu.SemaphoreType.DMA((len(streams), bits))] * (2 * phases),
         compiler_params=pltpu.CompilerParams(collective_id=call_id, has_side_effects=True),
         name="sum_whole" if whole else "sum_share",
-    )(*[array.reshape(split + (columns,)) for array in arrays])
+    )(*[array.reshape(split + (columns,)) for array in arrays], *added)
     shares = results[:count]
     return shares, [array.reshape(rows, columns) for array in results[count:]]
 
@@ -449,7 +497,7 @@
     inner_grads = sum_over_tok(local_grads, devices, 0, True)[1]
     news, *saved = unitary_forward(inner_grads, (w_gate, w_up, w_down))
     sums, query_stored = query_forward(news, queries, out_gain, cotangent)
-    sums = lax.psum(sums, "head")
+    sums = sum_over_pair(sums, lax.axis_size("head"), 3)
     query_grad, query_terms = query_backward(
         news, queries, out_gain, cotangent, sums, query_stored, full_width
     )
@@ -458,9 +506,9 @@
     key_grad, value_grad, key_terms = key_backward(
         w_gate, w_up, w_down, key_rows, step_rates, stored, cots
     )
-    key_shares, _ = sum_over_tok(key_terms, devices, 2, False)
+    weight_shares, _ = sum_over_tok(key_terms, devices, 2, False, query_shares)
     return (query_grad[None], key_grad[None], value_grad[None]) + tuple(
-        (query_share + key_share)[None] for query_share, key_share in zip(query_shares, key_shares)
+        share[None] for share in weight_shares
     )
 
 

time: 259 us -> 218 us (0.84)
  waiting for transfers between devices: 16.6 us -> 0 us
  between operations: 14.1 us -> 0.67 us
  Pallas kernels: 223 us -> 211 us
  local copies, waits for them, and re-layouts: 1.48 us -> 5.89 us
  other arithmetic: 3.01 us -> 0 us
    psum x1 -> x0, waiting for transfers between devices: 16.5 us -> none  [local(): sums = lax.psum(sums, 'head')]
    pallas_call x3 -> x4, Pallas kernels: 166 us -> 153 us  [the longest x3 150 us: sum_over_tok(): pl.pallas_call(kernel, out_shape=outs, in_specs=[vmem] * (count + len(add...]
    unnamed x6 -> x3, local copies, waits for them, and re-layouts: 0.01 us -> 4.42 us
    broadcast_in_dim x2 -> x0, other arithmetic: 3.01 us -> none  [local(): (query_share + key_share)[None]]
  transfers between devices with their start and end apart: 1 -> 0, of which waited for: 1 -> 0; matrix products, arithmetic and copies ran while one was open for 0% -> 0% of each run, Pallas kernels for 0% -> 0%
where the time goes in v1:
time: 218 us; the launch traced here: 217 us
  Pallas kernels  211 us (97%)
  local copies, waits for them, and re-layouts  5.89 us (3%)
    pallas_call x3, Pallas kernels, sum_over_tok(): pl.pallas_call(kernel, out_shape=outs, in_specs=[vmem] * (count + len(add...  150 us
    pallas_call x1, Pallas kernels, unitary_backward(): pl.pallas_call(kernel, grid=(count,), out_shape=jax.ShapeDtypeStruct((cou...  21.6 us
    pallas_call x4, Pallas kernels, on_core(): pl.pallas_call(kernel, out_shape=[jax.ShapeDtypeStruct(shape, kind) for s...  18.7 us
    pallas_call x1, Pallas kernels, unitary_forward(): pl.pallas_call(kernel, grid=(count,), out_shape=[jax.ShapeDtypeStruct((co...  16.9 us
    unnamed x3, local copies, waits for them, and re-layouts  4.42 us

profile of v1, /device:TPU:0, one launch (start us, length us, event | category | flops | bytes accessed | tf_op | source)
XLA Modules:
  0.0 217.3 jit_solution(17860438752056469231)
XLA Ops:
  0.6 1.5 copy.15.rates
  2.1 4.7 %key_forward.1 = (f32[512,512]{1,0:T(8,128)}, f32[512,512]{1,0:T(8,128)}, f32[512,512]{1,0:T(8,128)}, f32[256,512]{1,0:T(8,128)}, f32[256,512]{1,0:T(8,128)}, /*...) custom-call(bf16[512,512]{1,0:T(8,128)(2,1)} %bitcast.29, ...), custom_call_target="tpu_custom_call" | custom-call | tf_op jit(solution)/shard_map/key_forward/pallas_call | solution.py:139
  6.8 61.1 %sum_whole.2 = (f32[32,512]{1,0:T(8,128)}, f32[32,512]{1,0:T(8,128)}, f32[32,512]{1,0:T(8,128)}, f32[2,2,2,2,32,512]{5,4,3,2,1,0:T(8,128)}, f32[2,2,2,2,32,512]{...) custom-call(f32[2,2,2,2,32,512]{5,4,3,2,1,0:T(8,128)} %bitcast.50, f32[2,2,2,2,32,512]{5,4,3,2,1,0:T(8,128)} %bitcast.51, ...), custom_call_target="tpu_custom_call" | custom-call | tf_op jit(solution)/shard_map/sum_whole/pallas_call | solution.py:467
  67.9 16.9 %unitary_forward.1 = (bf16[3,512,512]{2,1,0:T(8,128)(2,1)}, bf16[3,3,512,512]{3,2,1,0:T(8,128)(2,1)}, bf16[3,3,512,512]{3,2,1,0:T(8,128)(2,1)}, bf16[3,3,512,512]{3,2,1,0:T(8,128)(2,1)}) custom-call(f32[512,512]{1,0:T(8,128)} %bitcast.38, f32[512,512]{1,0:T(8,128)} %bitcast.40, f32[512,512]{1,0:T(8,128)} %bitcast.42, bf16[512,512]{1,0:T(8,128)(2,1)} %bitcast.30, ...), custom_call_target="tpu_custom_call" | custom-call | tf_op jit(solution)/shard_map/unitary_forward/pallas_call | solution.py:73
  84.9 3.1 %query_forward.1 = (f32[256,128]{1,0:T(8,128)}, f32[256,512]{1,0:T(8,128)}, f32[256,512]{1,0:T(8,128)}, bf16[256,512]{1,0:T(8,128)(2,1)}, f32[256,512]{1,0:T(8,128)}) custom-call(bf16[3,512,512]{2,1,0:T(8,128)(2,1)} %get-tuple-element.52.news, bf16[256,512]{1,0:T(8,128)(2,1)} %bitcast.53, f32[1,512]{1,0:T(1,128)} %gain.3, bf16[256,512]{1,0:T(8,128)(2,1)} %bitcast.55), custom_call_target="tpu_custom_call" | custom-call | tf_op jit(solution)/shard_map/query_forward/pallas_call | solution.py:139
  88.0 2.9 %sum_pair.1.sums = f32[256,128]{1,0:T(8,128)} custom-call(f32[256,128]{1,0:T(8,128)} %get-tuple-element.53.given), custom_call_target="tpu_custom_call" | custom-call | tf_op jit(solution)/shard_map/sum_pair/pallas_call | solution.py:332
  90.9 4.8 %query_backward.1 = (bf16[256,512]{1,0:T(8,128)(2,1)}, f32[512,512]{1,0:T(8,128)}, f32[512,512]{1,0:T(8,128)}, f32[512,512]{1,0:T(8,128)}, bf16[256,512]{1,0:T(8...) custom-call(bf16[3,512,512]{2,1,0:T(8,128)(2,1)} %get-tuple-element.52.news, bf16[256,512]{1,0:T(8,128)(2,1)} %bitcast.54, ...), custom_call_target="tpu_custom_call" | custom-call | tf_op jit(solution)/shard_map/query_backward/pallas_call | solution.py:139
  95.6 58.1 %sum_whole.3 = (f32[32,512]{1,0:T(8,128)}, f32[32,512]{1,0:T(8,128)}, f32[32,512]{1,0:T(8,128)}, f32[2,2,2,2,32,512]{5,4,3,2,1,0:T(8,128)}, f32[2,2,2,2,32,512]{...) custom-call(f32[2,2,2,2,32,512]{5,4,3,2,1,0:T(8,128)} %bitcast.47, f32[2,2,2,2,32,512]{5,4,3,2,1,0:T(8,128)} %bitcast.48, ...), custom_call_target="tpu_custom_call" | custom-call | tf_op jit(solution)/shard_map/sum_whole/pallas_call | solution.py:467
  153.7 21.6 %unitary_backward.1.cots = bf16[3,512,512]{2,1,0:T(8,128)(2,1)} custom-call(f32[512,512]{1,0:T(8,128)} %bitcast.39, f32[512,512]{1,0:T(8,128)} %bitcast.41, f32[512,512]{1,0:T(8,128)} %bitcast.43, f32[512,512]{1,0:T(8,128)} %bitcast.59, f32[512,512]{1,0:T(8,128)} %bitcast.60, f32[512,512]{1,0:T(8,128)} %bitcast.61, ...), custom_call_target="tpu_custom_call" | custom-call | tf_op jit(solution)/shard_map/unitary_backward/pallas_call | solution.py:126
  175.3 6.2 %key_backward.1 = (bf16[256,512]{1,0:T(8,128)(2,1)}, bf16[256,512]{1,0:T(8,128)(2,1)}, f32[512,512]{1,0:T(8,128)}, f32[512,512]{1,0:T(8,128)}, f32[512,512]{1,0:...) custom-call(bf16[512,512]{1,0:T(8,128)(2,1)} %bitcast.31, ...), custom_call_target="tpu_custom_call" | custom-call | tf_op jit(solution)/shard_map/key_backward/pallas_call | solution.py:139
  181.5 31.3 %sum_share.1 = (f32[32,512]{1,0:T(8,128)}, f32[32,512]{1,0:T(8,128)}, f32[32,512]{1,0:T(8,128)}) custom-call(f32[2,2,2,2,32,512]{5,4,3,2,1,0:T(8,128)} %bitcast.44, f32[2,2,2,2,32,512]{5,4,3,2,1,0:T(8,128)} %bitcast.45, f32[2,2,2,2,32,512]{5,4,3,2,1,0:T(8,128)} %bitcast.46, f32[32,512]{1,0:T(8,128)} %get-tuple-element.80.refs_3_, ...), custom_call_target="tpu_custom_call" | custom-call | tf_op jit(solution)/shard_map/sum_share/pallas_call | solution.py:467
  212.8 1.5 copy.20
  214.3 1.5 copy.21
  215.8 1.5 copy.22

commit v2 on v1

--- a/solution.py
+++ b/solution.py
@@ -35,114 +35,119 @@
 def unitary_forward(inner_grads, weights):
     size = weights[0].shape[0]
     count = len(weights)
+    every = range(count)
 
     def kernel(*refs):
         matrices, olds = refs[:count], refs[count : 2 * count]
-        new_ref, narrow_ref, gram_ref, poly_ref, current = refs[2 * count :]
-        for which in range(count):
-
-            @pl.when(pl.program_id(0) == which)
-            def _(which=which):
-                matrix = matrices[which][...]
-                current[...] = matrix / jnp.sqrt(jnp.sum(matrix * matrix) + 1e-06)
+        new_ref, narrow_ref, gram_ref, poly_ref = refs[2 * count : 2 * count + 4]
+        current = refs[2 * count + 4 :]
+        for which in every:
+            matrix = matrices[which][...]
+            current[which][...] = matrix / jnp.sqrt(jnp.sum(matrix * matrix) + 1e-06)
 
         def step(iteration, carry):
-            narrow = current[...].astype(jnp.bfloat16)
-            narrow_ref[0, iteration] = narrow
-            gram = mxu(narrow, narrow, 1, 1)
-            gram_low = gram.astype(jnp.bfloat16)
-            gram_ref[0, iteration] = gram_low
-            poly = (coef_second * gram + coef_third * mxu(gram_low, gram_low, 1, 0)).astype(
-                jnp.bfloat16
-            )
-            poly_ref[0, iteration] = poly
-            current[...] = coef_first * current[...] + mxu(poly, narrow, 1, 0)
+            grams = []
+            for which in every:
+                narrow = current[which][...].astype(jnp.bfloat16)
+                narrow_ref[which, iteration] = narrow
+                grams.append(mxu(narrow, narrow, 1, 1))
+            for which in every:
+                gram_low = grams[which].astype(jnp.bfloat16)
+                gram_ref[which, iteration] = gram_low
+                poly_ref[which, iteration] = (
+                    coef_second * grams[which] + coef_third * mxu(gram_low, gram_low, 1, 0)
+                ).astype(jnp.bfloat16)
+            for which in every:
+                current[which][...] = coef_first * current[which][...] + mxu(
+                    poly_ref[which, iteration], narrow_ref[which, iteration], 1, 0
+                )
             return carry
 
         lax.fori_loop(0, NS_STEPS, step, 0)
-        for which in range(count):
-
-            @pl.when(pl.program_id(0) == which)
-            def _(which=which):
-                old = olds[which][...].astype(jnp.float32)
-                new_ref[0] = (old - inner_step * current[...]).astype(jnp.bfloat16)
-
-    vmem = pl.BlockSpec(memory_space=pltpu.VMEM)
-    saved = jax.ShapeDtypeStruct((count, NS_STEPS, size, size), jnp.bfloat16)
-    saved_spec = pl.BlockSpec((1, NS_STEPS, size, size), lambda i: (i, 0, 0, 0))
-    return pl.pallas_call(
-        kernel,
-        grid=(count,),
-        out_shape=[jax.ShapeDtypeStruct((count, size, size), jnp.bfloat16), saved, saved, saved],
-        in_specs=[vmem] * (2 * count),
-        out_specs=[pl.BlockSpec((1, size, size), lambda i: (i, 0, 0))] + [saved_spec] * 3,
-        scratch_shapes=[pltpu.VMEM((size, size), jnp.float32)],
-        name="unitary_forward",
-    )(*inner_grads, *weights)
+        for which in every:
+            old = olds[which][...].astype(jnp.float32)
+            new_ref[which] = (old - inner_step * current[which][...]).astype(jnp.bfloat16)
+
+    saved = ((count, NS_STEPS, size, size), jnp.bfloat16)
+    return on_core(
+        kernel,
+        "unitary_forward",
+        [((count, size, size), jnp.bfloat16), saved, saved, saved],
+        *inner_grads,
+        *weights,
+        scratch=[pltpu.VMEM((size, size), jnp.float32)] * count,
+    )
 
 
 def unitary_backward(inner_grads, outer_grads, saved):
     size = inner_grads[0].shape[0]
     count = len(inner_grads)
+    every = range(count)
 
     def kernel(*refs):
         matrices, outers = refs[:count], refs[count : 2 * count]
-        narrow_ref, gram_ref, poly_ref, cot_ref, grad = refs[2 * count :]
-        for which in range(count):
-
-            @pl.when(pl.program_id(0) == which)
-            def _(which=which):
-                grad[...] = -inner_step * outers[which][...]
+        narrow_ref, gram_ref, poly_ref, cot_ref = refs[2 * count : 2 * count + 4]
+        grad = refs[2 * count + 4 :]
+        for which in every:
+            grad[which][...] = -inner_step * outers[which][...]
 
         def step(back_iteration, carry):
             iteration = NS_STEPS - 1 - back_iteration
-            narrow = narrow_ref[0, iteration]
-            gram_low = gram_ref[0, iteration]
-            grad_low = grad[...].astype(jnp.bfloat16)
-            poly_grad = mxu(grad_low, narrow, 1, 1).astype(jnp.bfloat16).astype(jnp.float32)
-            pair = poly_grad + poly_grad.T
-            product = mxu(pair.astype(jnp.bfloat16), gram_low, 1, 0)
-            gram_grad = coef_second * pair + coef_third * (product + product.T)
-            narrow_grad = mxu(poly_ref[0, iteration], grad_low, 0, 0) + mxu(
-                gram_grad.astype(jnp.bfloat16), narrow, 1, 0
-            )
-            grad[...] = coef_first * grad[...] + narrow_grad.astype(jnp.bfloat16).astype(
-                jnp.float32
-            )
+            pairs = []
+            for which in every:
+                poly_grad = mxu(
+                    grad[which][...].astype(jnp.bfloat16), narrow_ref[which, iteration], 1, 1
+                )
+                poly_grad = poly_grad.astype(jnp.bfloat16).astype(jnp.float32)
+                pairs.append(poly_grad + poly_grad.T)
+            for which in every:
+                pair = pairs[which]
+                product = mxu(pair.astype(jnp.bfloat16), gram_ref[which, iteration], 1, 0)
+                pairs[which] = (
+                    coef_second * pair + coef_third * (product + product.T)
+                ).astype(jnp.bfloat16)
+            for which in every:
+                grad_low = grad[which][...].astype(jnp.bfloat16)
+                narrow_grad = mxu(poly_ref[which, iteration], grad_low, 1, 0) + mxu(
+                    pairs[which], narrow_ref[which, iteration], 1, 0
+                )
+                grad[which][...] = coef_first * grad[which][...] + narrow_grad.astype(
+                    jnp.bfloat16
+                ).astype(jnp.float32)
             return carry
 
         lax.fori_loop(0, NS_STEPS, step, 0)
-        for which in range(count):
-
-            @pl.when(pl.program_id(0) == which)
-            def _(which=which):
-                matrix = matrices[which][...]
-                inverse = lax.rsqrt(jnp.sum(matrix * matrix) + 1e-06)
-                along = jnp.sum(matrix * grad[...]) * inverse * inverse * inverse
-                cot_ref[0] = (grad[...] * inverse - matrix * along).astype(jnp.bfloat16)
-
-    vmem = pl.BlockSpec(memory_space=pltpu.VMEM)
-    saved_spec = pl.BlockSpec((1, NS_STEPS, size, size), lambda i: (i, 0, 0, 0))
-    return pl.pallas_call(
-        kernel,
-        grid=(count,),
-        out_shape=jax.ShapeDtypeStruct((count, size, size), jnp.bfloat16),
-        in_specs=[vmem] * (2 * count) + [saved_spec] * 3,
-        out_specs=pl.BlockSpec((1, size, size), lambda i: (i, 0, 0)),
-        scratch_shapes=[pltpu.VMEM((size, size), jnp.float32)],
-        name="unitary_backward",
-    )(*inner_grads, *outer_grads, *saved)
-
-
-def on_core(kernel, name, outs, *operands):
+        for which in every:
+            matrix = matrices[which][...]
+            inverse = lax.rsqrt(jnp.sum(matrix * matrix) + 1e-06)
+            along = jnp.sum(matrix * grad[which][...]) * inverse * inverse * inverse
+            cot_ref[which] = (grad[which][...] * inverse - matrix * along).astype(jnp.bfloat16)
+
+    return on_core(
+        kernel,
+        "unitary_backward",
+        [((count, size, size), jnp.bfloat16)],
+        *inner_grads,
+        *outer_grads,
+        *saved,
+        scratch=[pltpu.VMEM((size, size), jnp.float32)] * count,
+    )[0]
+
+
+def on_core(kernel, name, outs, *operands, scratch=()):
     vmem = pl.BlockSpec(memory_space=pltpu.VMEM)
     return pl.pallas_call(
         kernel,
         out_shape=[jax.ShapeDtypeStruct(shape, kind) for shape, kind in outs],
         in_specs=[vmem] * len(operands),
         out_specs=[vmem] * len(outs),
+        scratch_shapes=list(scratch),
         name=name,
     )(*operands)
+
+
+def column_of(row):
+    return jnp.broadcast_to(row, (128, row.shape[1])).T[:, :1]
 
 
 def key_forward(w_gate, w_up, w_down, key_rows, value_rows, step_rates):
@@ -150,7 +155,7 @@
         rows = keys[...]
         key_gate = mxu(rows, gate_w[...], 1, 0)
         key_up = mxu(rows, up_w[...], 1, 0)
-        aim = (-rates[...] * values[...].astype(jnp.float32)).astype(jnp.bfloat16)
+        aim = (-column_of(rates[...]) * values[...].astype(jnp.float32)).astype(jnp.bfloat16)
         key_mid = mxu(aim, down_w[...], 1, 1)
         act_gate, slope_gate, _ = silu_parts(key_gate)
         gate[...] = key_gate
@@ -175,7 +180,7 @@
         w_down,
         key_rows,
         value_rows,
-        step_rates[:, None],
+        step_rates[None],
     )
     return results[:3], results[3:]
 
@@ -213,7 +218,7 @@
             + mxu(up_low[...], up_w[...], 1, 1)
         ).astype(jnp.bfloat16)
         value_sum = mxu(mixed[...], cots[2], 1, 0) + mxu(mid_low[...], down_w[...], 1, 0)
-        value_grad[...] = (-rates[...] * value_sum).astype(jnp.bfloat16)
+        value_grad[...] = (-column_of(rates[...]) * value_sum).astype(jnp.bfloat16)
 
     square = (w_gate.shape, jnp.float32)
     narrow = (key_rows.shape, jnp.bfloat16)
@@ -225,11 +230,23 @@
         w_up,
         w_down,
         key_rows,
-        step_rates[:, None],
+        step_rates[None],
         *stored,
         cots,
     )
     return results[0], results[1], results[2:5]
+
+
+def add_shares(first, second):
+    count = len(first)
+
+    def kernel(*refs):
+        for which in range(count):
+            refs[2 * count + which][...] = refs[which][...] + refs[count + which][...]
+
+    return on_core(
+        kernel, "add_shares", [(share.shape, jnp.float32) for share in first], *first, *second
+    )
 
 
 def query_forward(news, queries, out_gain, cotangent):
@@ -350,7 +367,7 @@
     return tuple(plain[turn:] + plain[:turn] for turn in range(bits))
 
 
-def sum_over_tok(arrays, devices, call_id, whole, added=()):
+def sum_over_tok(arrays, devices, call_id, whole):
     bits = devices.bit_length() - 1
     rows, columns = arrays[0].shape
     block = rows // devices
@@ -366,10 +383,8 @@
 
     def kernel(*refs):
         given = refs[:count]
-        addends = refs[count : count + len(added)]
-        position = count + len(added)
-        shares = refs[position : position + count]
-        position += count
+        shares = refs[count : 2 * count]
+        position = 2 * count
         wholes = refs[position : position + count] if whole else ()
         position += len(wholes)
         partial = refs[position : position + count]
@@ -440,7 +455,7 @@
                 if step < bits:
                     partial[array][kept] = total
                 else:
-                    shares[array][:, lanes] = total + addends[array][:, lanes] if added else total
+                    shares[array][:, lanes] = total
                     if whole:
                         wholes[array][kept] = total
             if step < bits:
@@ -467,7 +482,7 @@
     results = pl.pallas_call(
         kernel,
         out_shape=outs,
-        in_specs=[vmem] * (count + len(added)),
+        in_specs=[vmem] * count,
         out_specs=[vmem] * len(outs),
         scratch_shapes=[pltpu.VMEM(split + (columns,), jnp.float32)] * count
         + [
@@ -477,7 +492,7 @@
         + [pltpu.SemaphoreType.DMA((len(streams), bits))] * (2 * phases),
         compiler_params=pltpu.CompilerParams(collective_id=call_id, has_side_effects=True),
         name="sum_whole" if whole else "sum_share",
-    )(*[array.reshape(split + (columns,)) for array in arrays], *added)
+    )(*[array.reshape(split + (columns,)) for array in arrays])
     shares = results[:count]
     return shares, [array.reshape(rows, columns) for array in results[count:]]
 
@@ -506,7 +521,8 @@
     key_grad, value_grad, key_terms = key_backward(
         w_gate, w_up, w_down, key_rows, step_rates, stored, cots
     )
-    weight_shares, _ = sum_over_tok(key_terms, devices, 2, False, query_shares)
+    key_shares, _ = sum_over_tok(key_terms, devices, 2, False)
+    weight_shares = add_shares(query_shares, key_shares)
     return (query_grad[None], key_grad[None], value_grad[None]) + tuple(
         share[None] for share in weight_shares
     )

time: 218 us -> 210 us (0.963)
  local copies, waits for them, and re-layouts: 5.89 us -> 0 us
    pallas_call x5 -> x3, Pallas kernels: 189 us -> 150 us  [sum_over_tok(): pl.pallas_call(kernel, out_shape=outs, in_specs=[vmem] * count, out_specs...]
    pallas_call x4 -> x7, Pallas kernels: 18.7 us -> 55.5 us  [on_core(): pl.pallas_call(kernel, out_shape=[jax.ShapeDtypeStruct(shape, kind) for s...]
    unnamed x3 -> x0, local copies, waits for them, and re-layouts: 4.42 us -> none
where the time goes in v2:
time: 210 us
  Pallas kernels  209 us (100%)
    pallas_call x3, Pallas kernels, sum_over_tok(): pl.pallas_call(kernel, out_shape=outs, in_specs=[vmem] * count, out_specs...  150 us
    pallas_call x7, Pallas kernels, on_core(): pl.pallas_call(kernel, out_shape=[jax.ShapeDtypeStruct(shape, kind) for s...  55.5 us

profile of v2, /device:TPU:0, one launch (start us, length us, event | category | flops | bytes accessed | tf_op | source)
XLA Modules:
  0.0 209.6 jit_solution(3134579982020702983)
XLA Ops:
  0.6 4.6 %key_forward.1 = (f32[512,512]{1,0:T(8,128)}, f32[512,512]{1,0:T(8,128)}, f32[512,512]{1,0:T(8,128)}, f32[256,512]{1,0:T(8,128)}, f32[256,512]{1,0:T(8,128)}, /*...) custom-call(bf16[512,512]{1,0:T(8,128)(2,1)} %bitcast.28, ...), custom_call_target="tpu_custom_call" | custom-call | tf_op jit(solution)/shard_map/key_forward/pallas_call | solution.py:139
  5.2 61.1 %sum_whole.2 = (f32[32,512]{1,0:T(8,128)}, f32[32,512]{1,0:T(8,128)}, f32[32,512]{1,0:T(8,128)}, f32[2,2,2,2,32,512]{5,4,3,2,1,0:T(8,128)}, f32[2,2,2,2,32,512]{...) custom-call(f32[2,2,2,2,32,512]{5,4,3,2,1,0:T(8,128)} %bitcast.49, f32[2,2,2,2,32,512]{5,4,3,2,1,0:T(8,128)} %bitcast.50, ...), custom_call_target="tpu_custom_call" | custom-call | tf_op jit(solution)/shard_map/sum_whole/pallas_call | solution.py:482
  66.3 15.0 %unitary_forward.1 = (bf16[3,512,512]{2,1,0:T(8,128)(2,1)}, bf16[3,3,512,512]{3,2,1,0:T(8,128)(2,1)}, bf16[3,3,512,512]{3,2,1,0:T(8,128)(2,1)}, bf16[3,3,512,512]{3,2,1,0:T(8,128)(2,1)}) custom-call(f32[512,512]{1,0:T(8,128)} %bitcast.37, f32[512,512]{1,0:T(8,128)} %bitcast.39, f32[512,512]{1,0:T(8,128)} %bitcast.41, bf16[512,512]{1,0:T(8,128)(2,1)} %bitcast.29, ...), custom_call_target="tpu_custom_call" | custom-call | tf_op jit(solution)/shard_map/unitary_forward/pallas_call | solution.py:139
  81.3 3.1 %query_forward.1 = (f32[256,128]{1,0:T(8,128)}, f32[256,512]{1,0:T(8,128)}, f32[256,512]{1,0:T(8,128)}, bf16[256,512]{1,0:T(8,128)(2,1)}, f32[256,512]{1,0:T(8,128)}) custom-call(bf16[3,512,512]{2,1,0:T(8,128)(2,1)} %get-tuple-element.55.news, bf16[256,512]{1,0:T(8,128)(2,1)} %bitcast.52, f32[1,512]{1,0:T(1,128)} %gain.3, bf16[256,512]{1,0:T(8,128)(2,1)} %bitcast.54), custom_call_target="tpu_custom_call" | custom-call | tf_op jit(solution)/shard_map/query_forward/pallas_call | solution.py:139
  84.4 2.9 %sum_pair.1.sums = f32[256,128]{1,0:T(8,128)} custom-call(f32[256,128]{1,0:T(8,128)} %get-tuple-element.56.given), custom_call_target="tpu_custom_call" | custom-call | tf_op jit(solution)/shard_map/sum_pair/pallas_call | solution.py:349
  87.3 4.7 %query_backward.1 = (bf16[256,512]{1,0:T(8,128)(2,1)}, f32[512,512]{1,0:T(8,128)}, f32[512,512]{1,0:T(8,128)}, f32[512,512]{1,0:T(8,128)}, bf16[256,512]{1,0:T(8...) custom-call(bf16[3,512,512]{2,1,0:T(8,128)(2,1)} %get-tuple-element.55.news, bf16[256,512]{1,0:T(8,128)(2,1)} %bitcast.53, ...), custom_call_target="tpu_custom_call" | custom-call | tf_op jit(solution)/shard_map/query_backward/pallas_call | solution.py:139
  92.1 58.0 %sum_whole.3 = (f32[32,512]{1,0:T(8,128)}, f32[32,512]{1,0:T(8,128)}, f32[32,512]{1,0:T(8,128)}, f32[2,2,2,2,32,512]{5,4,3,2,1,0:T(8,128)}, f32[2,2,2,2,32,512]{...) custom-call(f32[2,2,2,2,32,512]{5,4,3,2,1,0:T(8,128)} %bitcast.43, f32[2,2,2,2,32,512]{5,4,3,2,1,0:T(8,128)} %bitcast.44, ...), custom_call_target="tpu_custom_call" | custom-call | tf_op jit(solution)/shard_map/sum_whole/pallas_call | solution.py:482
  150.1 20.3 %unitary_backward.1.cots = bf16[3,512,512]{2,1,0:T(8,128)(2,1)} custom-call(f32[512,512]{1,0:T(8,128)} %bitcast.38, f32[512,512]{1,0:T(8,128)} %bitcast.40, f32[512,512]{1,0:T(8,128)} %bitcast.42, f32[512,512]{1,0:T(8,128)} %bitcast.58, f32[512,512]{1,0:T(8,128)} %bitcast.59, f32[512,512]{1,0:T(8,128)} %bitcast.60, ...), custom_call_target="tpu_custom_call" | custom-call | tf_op jit(solution)/shard_map/unitary_backward/pallas_call | solution.py:139
  170.5 6.1 %key_backward.1 = (bf16[256,512]{1,0:T(8,128)(2,1)}, bf16[256,512]{1,0:T(8,128)(2,1)}, f32[512,512]{1,0:T(8,128)}, f32[512,512]{1,0:T(8,128)}, f32[512,512]{1,0:...) custom-call(bf16[512,512]{1,0:T(8,128)(2,1)} %bitcast.30, ...), custom_call_target="tpu_custom_call" | custom-call | tf_op jit(solution)/shard_map/key_backward/pallas_call | solution.py:139
  176.6 31.3 %sum_share.1 = (f32[32,512]{1,0:T(8,128)}, f32[32,512]{1,0:T(8,128)}, f32[32,512]{1,0:T(8,128)}) custom-call(f32[2,2,2,2,32,512]{5,4,3,2,1,0:T(8,128)} %bitcast.46, f32[2,2,2,2,32,512]{5,4,3,2,1,0:T(8,128)} %bitcast.47, f32[2,2,2,2,32,512]{5,4,3,2,1,0:T(8,128)} %bitcast.48), custom_call_target="tpu_custom_call" | custom-call | tf_op jit(solution)/shard_map/sum_share/pallas_call | solution.py:482
  207.9 1.7 add_shares.1
